TPU v7x, 128 devices: a whole 4x4x4 slice. The times are simulated.
128 devices in a mesh: sector: 8 (over z, core), mode: 16 (over y, x).
Axes of the slice: x: 4, y: 4, z: 4, core: 2. Of those that a mesh axis runs over, the one named last changes fastest.
Arguments:
- modes: bfloat16 [256, 3, 32, 80, 128], P('mode', None, 'sector'), may hold values from -0.1875 to 0.1875
- thickness: float32 [32, 80, 128], P('sector'), may hold values from -6 to 6
- stiff_taps: float32 [27], replicated, may hold values from -1.25 to 1.25
- mass_taps: float32 [27], replicated, may hold values from 0.02 to 0.2
- eigenvalues: float32 [256], P('mode'), may hold values from 0.5 to 2
Outputs:
- sensitivity: float32 [256, 256], P('sector', 'mode')
All inputs are finite; a program needn't handle non-finite values.
Results may differ from a plain program's by a relative error of at most 0.0029.
Values may be sent and summed in bfloat16 or wider, within the bound.
A program may use at most 64 MiB of HBM per device.

v0:
```python
import jax
import jax.numpy as jnp
from jax import lax
from jax.sharding import PartitionSpec as P


def extended(cells, sides, width):
    for axis, dim in sides:
        count = lax.axis_size(axis)
        ends = count - 1
        head = lax.slice_in_dim(cells, 0, width, axis=dim)
        tail = lax.slice_in_dim(cells, cells.shape[dim] - width, cells.shape[dim], axis=dim)
        cells = jnp.concatenate(
            [
                lax.ppermute(tail, axis, [(i, (i + 1) % count) for i in range(ends)]),
                cells,
                lax.ppermute(head, axis, [((i + 1) % count, i) for i in range(ends)]),
            ],
            axis=dim,
        )
    return cells


def stencil(field, padded_thick, stiff_taps, mass_taps, lams):
    size_x = field.shape[2] - 2
    size_y = field.shape[3] - 2
    size_z = field.shape[4] - 2
    shape_out = (field.shape[0], field.shape[1], size_x, size_y, size_z)
    centre = padded_thick[1 : 1 + size_x, 1 : 1 + size_y, 1 : 1 + size_z]
    stiff_acc = jnp.zeros(shape_out, jnp.float32)
    mass_acc = jnp.zeros(shape_out, jnp.float32)
    for aoff in range(3):
        for boff in range(3):
            for doff in range(3):
                index = 9 * aoff + 3 * boff + doff
                coeff = 0.5 * (
                    centre
                    + padded_thick[aoff : aoff + size_x, boff : boff + size_y, doff : doff + size_z]
                )
                moved = (
                    coeff
                    * field[:, :, aoff : aoff + size_x, boff : boff + size_y, doff : doff + size_z]
                )
                stiff_acc = stiff_acc + stiff_taps[index] * moved
                mass_acc = mass_acc + mass_taps[index] * moved
    return (stiff_acc - lams[:, None, None, None, None] * mass_acc).astype(jnp.bfloat16)


def spread(whole):
    sectors = lax.axis_size("sector")
    groups = lax.axis_size("mode")
    total = whole.shape[0]
    arranged = whole.reshape(sectors, total // sectors, groups, total // groups)
    arranged = arranged.transpose(0, 2, 1, 3).reshape(
        sectors * groups * (total // sectors), total // groups
    )
    return lax.psum_scatter(arranged, ("sector", "mode"), scatter_dimension=0, tiled=True)


def on_device(modes, thickness, stiff_taps, mass_taps, eigenvalues):
    local_modes = modes.shape[0]
    size_z = modes.shape[4]
    thick_rim = extended(thickness, (("sector", 0),), 1)
    padded_thick = jnp.pad(thick_rim, ((0, 0), (1, 1), (1, 1)))
    planes = extended(modes, (("sector", 2),), 1)
    field = jnp.pad(planes.astype(jnp.float32), ((0, 0), (0, 0), (0, 0), (1, 1), (1, 1)))
    loaded = stencil(field, padded_thick, stiff_taps, mass_taps, eigenvalues)
    flat_modes = modes.reshape(local_modes, -1, size_z)
    flat_loaded = loaded.reshape(local_modes, -1, size_z)
    all_modes, all_loaded = (
        lax.all_to_all(flat_modes, "mode", split_axis=1, concat_axis=0, tiled=True),
        lax.all_to_all(flat_loaded, "mode", split_axis=1, concat_axis=0, tiled=True),
    )
    whole = lax.dot_general(
        all_modes, all_loaded, (((1, 2), (1, 2)), ((), ())), preferred_element_type=jnp.float32
    )
    return spread(whole)


def solution(mesh):
    in_specs = (P("mode", None, "sector", None, None), P("sector", None, None), P(), P(), P("mode"))
    out_specs = P("sector", "mode")
    return jax.shard_map(
        on_device, mesh=mesh, in_specs=in_specs, out_specs=out_specs, check_vma=False
    )
```

profile of v0, /device:TPU:0, one launch (start us, length us, event | category | flops | bytes accessed | tf_op | source)
XLA Modules:
  0.0 861.1 jit_solution(12675278944696315850)
XLA Ops:
  6.5 0.8 fusion.56
  7.3 1.3 collective-permute-start
  8.6 1.3 collective-permute-start.1
  9.9 2.6 fusion.55
  12.6 5.3 collective-permute-start.2
  17.9 0.0 copy-start.3
  17.9 0.0 copy-start.4
  17.9 1.4 collective-permute-start.3
  19.4 6.5 copy.14
  25.9 7.1 all-to-all-start.1
  33.0 0.0 copy-start
  33.0 0.7 fusion.57
  33.7 0.7 fusion.58
  34.4 0.7 fusion.59
  35.2 0.7 fusion.60
  35.9 0.2 select_maximum_fusion
  36.1 0.2 fusion.53
  36.3 0.6 fusion.54
  37.0 0.9 maximum_convert_fusion
  38.0 96.1 %subtract_convert_fusion = bf16[16,3,4,80,128]{4,3,2,1,0:T(8,128)(2,1)S(1)} fusion(f32[16,3,6,80,128]{4,3,2,1,0:T(8,128)S(1)} %maximum_convert_fusion, f32[]{:T(128)} %bitcast.53, f32[]{:T(128)} %bitcast.52, f32[]{:T(128)} %bitcast.51, f32[]{:T(128)} %bitcast.50, f32[]{:T(128)} %bitcast.49, f32[]{:T(128)} %bitcast.48, f32[]{:T(128)} %bitcast.47, ...), kind=kLoop, calls=%fused_computation.51 | loop fusion | flops 267386880 | bytes 43746008 | tf_op jit(solution)/shard_map/convert_element_type | solution.py:46
  134.0 4.5 copy.12
  138.5 7.2 all-to-all-start
  145.7 0.0 reduce-scatter.4.cloned.1.call-start
  145.8 5.2 copy.15
  151.0 56.3 %all-to-all-done = bf16[16,960,128]{2,0,1:T(8,128)(2,1)} async-done(((bf16[16,960,128]{2,0,1:T(8,128)(2,1)}), bf16[16,960,128]{2,0,1:T(8,128)(2,1)}, u32[]{:S(2)}, u32[]{:S(2)}) %all-to-all-start) | async-done | bytes 3932192 | tf_op jit(solution)/shard_map/all_to_all | solution.py:72
  207.2 3.4 copy.13
  210.6 1.2 convolution_bitcast_fusion
  211.9 0.3 reshape.42
  212.1 2.0 copy.19
  214.1 0.0 reduce-scatter.4.cloned.1.call-update
  214.2 638.7 %reduce-scatter.4.cloned.1.call-done = f32[32,16]{1,0:T(8,128)} async-done(((f32[4096,16]{1,0:T(8,128)}), f32[32,16]{1,0:T(8,128)}) %reduce-scatter.4.cloned.1.call-update) | async-done | bytes 2064
  852.9 1.4 copy.18
  (14 shorter events, 0.0 us)
Async XLA Ops:
  7.3 28.5 %collective-permute-start = (f32[1,80,128]{2,1,0:T(8,128)S(1)}, f32[1,80,128]{2,1,0:T(8,128)S(1)}, u32[]{:S(2)}, u32[]{:S(2)}) collective-permute-start(f32[1,80,128]{2,1,0:T(8,128)S(1)} %get-tuple-element.34), channel_id=1, source_target_pairs={{0,16},{16,32},{32,48},{48,64},{64,80},{80,96},{96,112},{1,17},{17... | collective-permute-start | bytes 122888 | tf_op jit(solution)/shard_map/ppermute | solution.py:15
  8.6 27.2 %collective-permute-start.1 = (f32[1,80,128]{2,1,0:T(8,128)S(1)}, f32[1,80,128]{2,1,0:T(8,128)S(1)}, u32[]{:S(2)}, u32[]{:S(2)}) collective-permute-start(f32[1,80,128]{2,1,0:T(8,128)S(1)} %get-tuple-element.35), channel_id=1, source_target_pairs={{16,0},{32,16},{48,32},{64,48},{80,64},{96,80},{112,96},{17,1},{33... | collective-permute-start | bytes 122888 | tf_op jit(solution)/shard_map/ppermute | solution.py:17
  12.6 24.4 %collective-permute-start.2 = (bf16[16,3,1,80,128]{4,3,2,1,0:T(8,128)(2,1)}, bf16[16,3,1,80,128]{4,3,2,1,0:T(8,128)(2,1)S(1)}, u32[]{:S(2)}, u32[]{:S(2)}) collective-permute-start(bf16[16,3,1,80,128]{4,3,2,1,0:T(8,128)(2,1)} %get-tuple-element.5), channel_id=1, source_target_pairs={{0,16},{16,32},{32,48},{48,64},{64,80},{80,96},{96,112},{1,17},{17... | collective-permute-start | bytes 2949128 | tf_op jit(solution)/shard_map/ppermute | solution.py:15
  17.9 15.1 %copy-start.3 = (f32[27]{0:T(128)S(1)}, f32[27]{0:T(128)}, u32[]{:S(2)}) copy-start(f32[27]{0:T(128)} %param.7) | copy-start | bytes 328
  17.9 16.5 %copy-start.4 = (f32[27]{0:T(128)S(1)}, f32[27]{0:T(128)}, u32[]{:S(2)}) copy-start(f32[27]{0:T(128)} %param.8) | copy-start | bytes 328
  17.9 17.9 %copy-start.2 = (f32[4,80,128]{2,1,0:T(8,128)S(1)}, f32[4,80,128]{2,1,0:T(8,128)}, u32[]{:S(2)}) copy-start(f32[4,80,128]{2,1,0:T(8,128)} %param.6) | copy-start | bytes 491524
  17.9 19.1 %collective-permute-start.3 = (bf16[16,3,1,80,128]{4,3,2,1,0:T(8,128)(2,1)S(1)}, bf16[16,3,1,80,128]{4,3,2,1,0:T(8,128)(2,1)S(1)}, u32[]{:S(2)}, u32[]{:S(2)}) collective-permute-start(bf16[16,3,1,80,128]{4,3,2,1,0:T(8,128)(2,1)S(1)} %get-tuple-element.6), channel_id=1, source_target_pairs={{16,0},{32,16},{48,32},{64,48},{80,64},{96,80},{112,96},{17,1},{33... | collective-permute-start | bytes 2949128 | tf_op jit(solution)/shard_map/ppermute | solution.py:17
  25.9 112.6 %all-to-all-start.1 = ((bf16[16,960,128]{2,0,1:T(8,128)(2,1)}), bf16[16,960,128]{2,0,1:T(8,128)(2,1)}, u32[]{:S(2)}, u32[]{:S(2)}) async-start(bf16[16,960,128]{2,0,1:T(8,128)(2,1)} %bitcast.75), calls=%async_computation.1 | async-start | bytes 7864320 | tf_op jit(solution)/shard_map/all_to_all | solution.py:71
  33.0 4.0 copy-start
  37.0 1.0 copy-start.5
  138.5 68.7 %all-to-all-start = ((bf16[16,960,128]{2,0,1:T(8,128)(2,1)}), bf16[16,960,128]{2,0,1:T(8,128)(2,1)}, u32[]{:S(2)}, u32[]{:S(2)}) async-start(bf16[16,960,128]{2,0,1:T(8,128)(2,1)} %bitcast.76), calls=%async_computation | async-start | bytes 7864320 | tf_op jit(solution)/shard_map/all_to_all | solution.py:72
  145.7 707.1 %reduce-scatter.4.cloned.1.call-start = ((), (), s32[]{:S(2)}) async-start(), calls=%async_computation.3 | async-start | bytes 2113536
  207.2 3.4 copy-start.1
Sparse Core Ops, SparseCore 0:
  214.3 638.5 reduce-scatter.3
where the time goes:
time: 862 us; the launch traced here: 861 us
  waiting for transfers between devices  695 us (81%)
  other arithmetic  98.1 us (11%)
  local copies, waits for them, and re-layouts  29.5 us (3%)
  starting transfers between devices  23.6 us (3%)
  between operations  13.6 us (2%)
    unnamed x2, waiting for transfers between devices  639 us
    convert_element_type x1, other arithmetic, stencil(): (stiff_acc - lams[:, None, None, None, None] * mass_acc).astype(jnp.bfloa...  96.1 us
    all_to_all x1, waiting for transfers between devices, on_device(): lax.all_to_all(flat_loaded, 'mode', split_axis=1, concat_axis=0, tiled=True)  56.3 us
  transfers between devices with their start and end apart: 7, of which 2 were waited for; matrix products, arithmetic and copies ran while one was open for 14% of the time, Pallas kernels for 0%

commit v1 on v0

--- a/solution.py
+++ b/solution.py
@@ -69,7 +69,12 @@
     flat_loaded = loaded.reshape(local_modes, -1, size_z)
     all_modes, all_loaded = (
         lax.all_to_all(flat_modes, "mode", split_axis=1, concat_axis=0, tiled=True),
-        lax.all_to_all(flat_loaded, "mode", split_axis=1, concat_axis=0, tiled=True),
+        jnp.concatenate(
+            lax.all_to_all(
+                jnp.stack(jnp.split(flat_loaded, lax.axis_size("mode"), axis=1)), "mode", 0, 0
+            ),
+            axis=0,
+        ),
     )
     whole = lax.dot_general(
         all_modes, all_loaded, (((1, 2), (1, 2)), ((), ())), preferred_element_type=jnp.float32

time: 862 us -> 872 us (1.012)
  local copies, waits for them, and re-layouts: 29.5 us -> 39.1 us
    unnamed x15 -> x30, local copies, waits for them, and re-layouts: 9.95 us -> 20.7 us
  transfers between devices with their start and end apart: 7 -> 7, of which waited for: 2 -> 2; matrix products, arithmetic and copies ran while one was open for 14% -> 15% of each run, Pallas kernels for 0% -> 0%
where the time goes in v1:
time: 872 us; the launch traced here: 871 us
  waiting for transfers between devices  695 us (80%)
  other arithmetic  98.1 us (11%)
  local copies, waits for them, and re-layouts  39.1 us (4%)
  starting transfers between devices  23.9 us (3%)
  between operations  13.6 us (2%)
    unnamed x2, waiting for transfers between devices  639 us
    convert_element_type x1, other arithmetic, stencil(): (stiff_acc - lams[:, None, None, None, None] * mass_acc).astype(jnp.bfloa...  96.1 us
    all_to_all x1, waiting for transfers between devices, on_device(): lax.all_to_all(jnp.stack(jnp.split(flat_loaded, lax.axis_size('mode'), ax...  56 us
    unnamed x30, local copies, waits for them, and re-layouts  20.7 us
  transfers between devices with their start and end apart: 7, of which 2 were waited for; matrix products, arithmetic and copies ran while one was open for 15% of the time, Pallas kernels for 0%

profile of v1, /device:TPU:0, one launch (start us, length us, event | category | flops | bytes accessed | tf_op | source)
XLA Modules:
  0.0 870.6 jit_solution(18077665067913680038)
XLA Ops:
  6.5 0.8 fusion.72
  7.3 1.3 collective-permute-start
  8.6 1.3 collective-permute-start.1
  9.9 2.6 fusion.71
  12.6 5.3 collective-permute-start.2
  17.9 1.4 collective-permute-start.3
  19.4 6.5 copy.44
  25.9 7.1 all-to-all-start.1
  33.0 0.7 fusion.73
  34.4 0.7 fusion.75
  37.0 0.9 maximum_convert_fusion
  38.0 96.1 %subtract_convert_fusion = bf16[16,3,4,80,128]{4,3,2,1,0:T(8,128)(2,1)S(1)} fusion(f32[16,3,6,80,128]{4,3,2,1,0:T(8,128)S(1)} %maximum_convert_fusion, f32[]{:T(128)} %bitcast.53, f32[]{:T(128)} %bitcast.52, f32[]{:T(128)} %bitcast.51, f32[]{:T(128)} %bitcast.50, f32[]{:T(128)} %bitcast.49, f32[]{:T(128)} %bitcast.48, f32[]{:T(128)} %bitcast.47, ...), kind=kLoop, calls=%fused_computation.51 | loop fusion | flops 267386880 | bytes 43746008 | tf_op jit(solution)/shard_map/convert_element_type | solution.py:46
  134.0 2.5 copy.42
  138.0 0.7 fusion.40
  138.7 0.7 fusion.39
  139.4 0.7 fusion.38
  140.2 0.7 fusion.37
  142.3 0.7 fusion.34
  143.0 0.7 fusion.33
  143.7 0.7 fusion.32
  144.5 0.7 fusion.31
  145.9 0.7 fusion.29
  146.6 0.7 fusion.28
  147.3 0.7 fusion.27
  148.0 7.2 all-to-all-start
  155.5 5.2 copy.45
  160.7 56.0 %all-to-all-done = bf16[16,16,60,128]{3,1,2,0:T(8,128)(2,1)} async-done(((bf16[16,16,60,128]{3,1,2,0:T(8,128)(2,1)}), bf16[16,16,60,128]{3,1,2,0:T(8,128)(2,1)}, u32[]{:S(2)}, u32[]{:S(2)}) %all-to-all-start) | async-done | bytes 3932192 | tf_op jit(solution)/shard_map/all_to_all | solution.py:73
  216.7 3.4 copy.43
  220.2 1.2 convolution_bitcast_fusion
  221.7 2.0 copy.49
  223.7 638.7 %reduce-scatter.4.cloned.1.call-done = f32[32,16]{1,0:T(8,128)} async-done(((f32[4096,16]{1,0:T(8,128)}), f32[32,16]{1,0:T(8,128)}) %reduce-scatter.4.cloned.1.call-update) | async-done | bytes 2064
  862.4 1.4 copy.48
  (30 shorter events, 6.6 us)
Async XLA Ops:
  7.3 28.5 %collective-permute-start = (f32[1,80,128]{2,1,0:T(8,128)S(1)}, f32[1,80,128]{2,1,0:T(8,128)S(1)}, u32[]{:S(2)}, u32[]{:S(2)}) collective-permute-start(f32[1,80,128]{2,1,0:T(8,128)S(1)} %get-tuple-element.34), channel_id=1, source_target_pairs={{0,16},{16,32},{32,48},{48,64},{64,80},{80,96},{96,112},{1,17},{17... | collective-permute-start | bytes 122888 | tf_op jit(solution)/shard_map/ppermute | solution.py:15
  8.6 27.2 %collective-permute-start.1 = (f32[1,80,128]{2,1,0:T(8,128)S(1)}, f32[1,80,128]{2,1,0:T(8,128)S(1)}, u32[]{:S(2)}, u32[]{:S(2)}) collective-permute-start(f32[1,80,128]{2,1,0:T(8,128)S(1)} %get-tuple-element.35), channel_id=1, source_target_pairs={{16,0},{32,16},{48,32},{64,48},{80,64},{96,80},{112,96},{17,1},{33... | collective-permute-start | bytes 122888 | tf_op jit(solution)/shard_map/ppermute | solution.py:17
  12.6 24.4 %collective-permute-start.2 = (bf16[16,3,1,80,128]{4,3,2,1,0:T(8,128)(2,1)}, bf16[16,3,1,80,128]{4,3,2,1,0:T(8,128)(2,1)S(1)}, u32[]{:S(2)}, u32[]{:S(2)}) collective-permute-start(bf16[16,3,1,80,128]{4,3,2,1,0:T(8,128)(2,1)} %get-tuple-element.5), channel_id=1, source_target_pairs={{0,16},{16,32},{32,48},{48,64},{64,80},{80,96},{96,112},{1,17},{17... | collective-permute-start | bytes 2949128 | tf_op jit(solution)/shard_map/ppermute | solution.py:15
  17.9 15.1 %copy-start.3 = (f32[27]{0:T(128)S(1)}, f32[27]{0:T(128)}, u32[]{:S(2)}) copy-start(f32[27]{0:T(128)} %param.7) | copy-start | bytes 328
  17.9 16.5 %copy-start.4 = (f32[27]{0:T(128)S(1)}, f32[27]{0:T(128)}, u32[]{:S(2)}) copy-start(f32[27]{0:T(128)} %param.8) | copy-start | bytes 328
  17.9 17.9 %copy-start.2 = (f32[4,80,128]{2,1,0:T(8,128)S(1)}, f32[4,80,128]{2,1,0:T(8,128)}, u32[]{:S(2)}) copy-start(f32[4,80,128]{2,1,0:T(8,128)} %param.6) | copy-start | bytes 491524
  17.9 19.1 %collective-permute-start.3 = (bf16[16,3,1,80,128]{4,3,2,1,0:T(8,128)(2,1)S(1)}, bf16[16,3,1,80,128]{4,3,2,1,0:T(8,128)(2,1)S(1)}, u32[]{:S(2)}, u32[]{:S(2)}) collective-permute-start(bf16[16,3,1,80,128]{4,3,2,1,0:T(8,128)(2,1)S(1)} %get-tuple-element.6), channel_id=1, source_target_pairs={{16,0},{32,16},{48,32},{64,48},{80,64},{96,80},{112,96},{17,1},{33... | collective-permute-start | bytes 2949128 | tf_op jit(solution)/shard_map/ppermute | solution.py:17
  25.9 122.2 %all-to-all-start.1 = ((bf16[16,960,128]{2,0,1:T(8,128)(2,1)}), bf16[16,960,128]{2,0,1:T(8,128)(2,1)}, u32[]{:S(2)}, u32[]{:S(2)}) async-start(bf16[16,960,128]{2,0,1:T(8,128)(2,1)} %bitcast.136), calls=%async_computation.1 | async-start | bytes 7864320 | tf_op jit(solution)/shard_map/all_to_all | solution.py:71
  33.0 4.0 copy-start
  37.0 1.0 copy-start.5
  148.0 68.7 %all-to-all-start = ((bf16[16,16,60,128]{3,1,2,0:T(8,128)(2,1)}), bf16[16,16,60,128]{3,1,2,0:T(8,128)(2,1)}, u32[]{:S(2)}, u32[]{:S(2)}) async-start(bf16[16,16,60,128]{3,1,2,0:T(8,128)(2,1)} %fusion.27), calls=%async_computation | async-start | bytes 7864320 | tf_op jit(solution)/shard_map/all_to_all | solution.py:73
  155.3 707.2 %reduce-scatter.4.cloned.1.call-start = ((), (), s32[]{:S(2)}) async-start(), calls=%async_computation.3 | async-start | bytes 2113536
  216.7 3.4 copy-start.1
Sparse Core Ops, SparseCore 0:
  223.8 638.5 reduce-scatter.3
